TPU v7x, 32 devices: a whole 2x2x4 slice. The times are simulated.
32 devices in a mesh: occ: 4 (over z), va: 2 (over x), vb: 4 (over y, core).
Axes of the slice: x: 2, y: 2, z: 4, core: 2. Of those that a mesh axis runs over, the one named last changes fastest.
Arguments:
- aux_factors: bfloat16 [4, 1024, 2048], P('occ', ('vb', 'va')), may hold values from -0.59765625 to 0.59765625
- occ_energy: float32 [4], replicated, may hold values from -2 to -0.5
- vir_energy: float32 [1024], replicated, may hold values from 0.5 to 3
- occ_index: int32 [4], replicated, may hold values from 0 to 3, each once
- vir_index: int32 [1024], replicated, may hold values from 0 to 1023, each once
Outputs:
- gamma_aux: float32 [4, 1024, 2048], P('occ', ('vb', 'va'))
Inputs may be any that keep to these rules, and one draw needn't show every extreme that they name: `occ_index`: each occupied table row appears exactly once. `vir_index`: each virtual table row appears exactly once.
All inputs are finite; a program needn't handle non-finite values.
Results may differ from a plain program's by a relative error of at most 0.0017.
Values may be sent and summed in bfloat16 or wider, within the bound.
No kernel may reach another device: no remote copies, remote signals or barrier semaphores. Data moves between devices by JAX's collectives and lax.ppermute only.
A program may use at most 64 MiB of HBM per device.

v0:
```python
import jax
import jax.numpy as jnp
from jax import lax
from jax.sharding import PartitionSpec as P

STEPS = 4


def passed_along(block, axis, distance):
    devices = range(lax.axis_size(axis))
    route = [((i - distance) % len(devices), i) for i in devices]
    return lax.ppermute(block, axis, route)


def lookup(indices, energies):
    positions = jnp.arange(energies.shape[0], dtype=jnp.int32)
    matches = indices[:, None] == positions[None, :]
    return jnp.sum(jnp.where(matches, energies[None, :], 0.0), axis=1)


def per_device(aux_factors, occ_energy, vir_energy, occ_index, vir_index):
    va_count = lax.axis_size("va")
    vb_count = lax.axis_size("vb")
    occ_count = lax.axis_size("occ")
    va_rank = lax.axis_index("va")
    vb_rank = lax.axis_index("vb")
    occ_rank = lax.axis_index("occ")
    occ_rows, block_width, aux_width = aux_factors.shape
    vir_width = vir_index.shape[0]
    row_count = vb_count * block_width
    col_count = va_count * block_width
    row_index = lax.dynamic_index_in_dim(
        vir_index.reshape(vb_count, va_count, block_width), va_rank, 1, False
    ).reshape(row_count)
    col_index = lax.dynamic_index_in_dim(
        vir_index.reshape(vb_count, vir_width // vb_count), vb_rank, 0, False
    )
    row_energy = lookup(row_index, vir_energy)
    col_energy = lookup(col_index, vir_energy)

    def block_energy(block_id):
        return lookup(
            lax.dynamic_slice_in_dim(occ_index, block_id * occ_rows, occ_rows), occ_energy
        )

    own_energy = block_energy(occ_rank)
    own_columns = lax.all_gather(aux_factors, "va", axis=1, tiled=True)
    own_rows = lax.all_gather(aux_factors, "vb", axis=1, tiled=True)
    gradient = jnp.zeros((occ_rows, row_count, aux_width), jnp.float32)
    far_columns = own_columns
    for distance in range(STEPS):
        if distance > 0:
            far_columns = passed_along(far_columns, "occ", 1)
        far_block = (occ_rank - distance + occ_count) % occ_count
        kernel = jnp.einsum(
            "iap,jbp->iajb", own_rows, far_columns, preferred_element_type=jnp.float32
        )
        outgoing = kernel.reshape(occ_rows, vb_count, block_width, occ_rows, va_count, block_width)
        outgoing = outgoing.transpose(4, 1, 0, 2, 3, 5).reshape(
            va_count * vb_count, occ_rows, block_width, occ_rows, block_width
        )
        incoming = lax.all_to_all(outgoing, ("va", "vb"), split_axis=0, concat_axis=0, tiled=True)
        incoming = incoming.reshape(
            va_count, vb_count, occ_rows, block_width, occ_rows, block_width
        )
        swapped = incoming.transpose(2, 1, 5, 4, 0, 3).reshape(
            occ_rows, row_count, occ_rows, col_count
        )
        energy_gap = (
            own_energy[:, None, None, None]
            + block_energy(far_block)[None, None, :, None]
            - row_energy[None, :, None, None]
            - col_energy[None, None, None, :]
        )
        weights = ((2.0 * kernel - swapped) / energy_gap).astype(jnp.bfloat16)
        gradient = gradient + jnp.einsum(
            "iajb,jbp->iap", weights, far_columns, preferred_element_type=jnp.float32
        )
    return lax.psum_scatter(gradient, "vb", scatter_dimension=1, tiled=True)


def solution(mesh):
    return jax.shard_map(
        per_device,
        mesh=mesh,
        in_specs=(P("occ", ("vb", "va"), None), P(), P(), P(), P()),
        out_specs=P("occ", ("vb", "va"), None),
        check_vma=False,
    )
```

profile of v0, /device:TPU:0, one launch (start us, length us, event | category | flops | bytes accessed | tf_op | source)
XLA Modules:
  0.0 195.6 jit_solution(13095508665357366006)
XLA Ops:
  6.5 0.7 all-gather.5.cloned.1.call-update
  7.3 0.0 all-gather.3.cloned.1.call-start
  7.3 0.7 all-gather.3.cloned.1.call-update
  8.0 24.9 %all-gather.5.cloned.1.call-done = bf16[1,256,2048]{2,1,0:T(8,128)(2,1)} async-done(((bf16[1,128,2048]{2,1,0:T(8,128)(2,1)}), bf16[1,256,2048]{2,1,0:T(8,128)(2,1)}) %all-gather.5.cloned.1.call-update) | async-done | bytes 1048592 | tf_op jit(solution)/shard_map/all_gather | solution.py:47
  32.9 1.5 collective-permute-start
  34.4 25.3 %collective-permute-done = bf16[1,256,2048]{2,1,0:T(8,128)(2,1)S(1)} collective-permute-done((bf16[1,256,2048]{2,1,0:T(8,128)(2,1)}, bf16[1,256,2048]{2,1,0:T(8,128)(2,1)S(1)}, u32[]{:S(2)}, u32[]{:S(2)}) %collective-permute-start) | collective-permute-done | bytes 1048608 | tf_op jit(solution)/shard_map/ppermute | solution.py:12
  59.7 0.0 collective-permute-start.1
  59.7 1.6 fusion.52
  61.2 4.4 %fusion.47 = (f32[]{:T(128)}, f32[]{:T(128)}, f32[]{:T(128)}, f32[]{:T(128)}, f32[]{:T(128)}) fusion(f32[4]{0:T(128)} %param.6, s32[]{:T(128)} %bitcast.32, s32[]{:T(128)} %bitcast.18, s32[]{:T(128)} %bitcast.8, s32[]{:T(128)} %bitcast.7, s32[]{:T(128)} %bitcast.25), kind=kLoop, calls=%fused_computation.61 | loop fusion | flops 55 | bytes 56 | tf_op jit(solution)/shard_map/reduce_sum | solution.py:18
  70.6 0.7 reshape.218
  71.3 0.7 constant_dynamic-slice_fusion.1
  72.0 1.0 select_reduce_fusion
  73.1 12.3 %collective-permute-done.1 = bf16[1,256,2048]{2,1,0:T(8,128)(2,1)S(1)} collective-permute-done((bf16[1,256,2048]{2,1,0:T(8,128)(2,1)S(1)}, bf16[1,256,2048]{2,1,0:T(8,128)(2,1)S(1)}, u32[]{:S(2)}, u32[]{:S(2)}) %collective-permute-start.1) | collective-permute-done | bytes 1048608 | tf_op jit(solution)/shard_map/ppermute | solution.py:12
  85.3 2.7 %fusion.2 = f32[512,256]{1,0:T(8,128)S(1)} fusion(bf16[1,512,2048]{2,1,0:T(8,128)(2,1)} %all-gather.3.cloned.1.call-done, bf16[1,256,2048]{2,1,0:T(8,128)(2,1)S(1)} %collective-permute-done.1), kind=kOutput, calls=%fused_computation.3 | convolution fusion | flops 536870912 | bytes 3670016 | tf_op jit(solution)/shard_map/iap,jbp->iajb/dot_general | solution.py:55
  88.1 0.3 reshape.225
  88.3 0.8 copy.32
  89.2 3.5 %all-to-all-start.2 = ((f32[8,1,128,1,128]{4,2,3,1,0:T(8,128)}), f32[8,1,128,1,128]{4,2,3,1,0:T(8,128)S(1)}, u32[]{:S(2)}, u32[]{:S(2)}) async-start(f32[8,1,128,1,128]{4,2,3,1,0:T(8,128)} %bitcast.22), calls=%async_computation.2 | async-start | bytes 1048576 | tf_op jit(solution)/shard_map/all_to_all | solution.py:62
  92.7 0.1 collective-permute-start.2
  92.8 2.3 %fusion.4 = f32[512,256]{1,0:T(8,128)S(1)} fusion(bf16[1,512,2048]{2,1,0:T(8,128)(2,1)} %all-gather.3.cloned.1.call-done, bf16[1,256,2048]{2,1,0:T(8,128)(2,1)S(1)} %collective-permute-done), kind=kOutput, calls=%fused_computation.5 | convolution fusion | flops 536870912 | bytes 3670016 | tf_op jit(solution)/shard_map/iap,jbp->iajb/dot_general | solution.py:55
  95.1 0.0 copy-start.2
  95.1 0.3 reshape.220
  95.4 0.8 copy.29
  96.2 5.2 %all-to-all-done.2 = f32[8,1,128,1,128]{4,2,3,1,0:T(8,128)S(1)} async-done(((f32[8,1,128,1,128]{4,2,3,1,0:T(8,128)}), f32[8,1,128,1,128]{4,2,3,1,0:T(8,128)S(1)}, u32[]{:S(2)}, u32[]{:S(2)}) %all-to-all-start.2) | async-done | bytes 524320 | tf_op jit(solution)/shard_map/all_to_all | solution.py:62
  101.5 3.5 %all-to-all-start.1 = ((f32[8,1,128,1,128]{4,2,3,1,0:T(8,128)}), f32[8,1,128,1,128]{4,2,3,1,0:T(8,128)S(1)}, u32[]{:S(2)}, u32[]{:S(2)}) async-start(f32[8,1,128,1,128]{4,2,3,1,0:T(8,128)} %bitcast.15), calls=%async_computation.1 | async-start | bytes 1048576 | tf_op jit(solution)/shard_map/all_to_all | solution.py:62
  105.0 0.2 select_reduce_fusion.1
  105.2 2.6 %fusion.6 = f32[512,256]{1,0:T(8,128)S(1)} fusion(bf16[1,512,2048]{2,1,0:T(8,128)(2,1)} %all-gather.3.cloned.1.call-done, bf16[1,256,2048]{2,1,0:T(8,128)(2,1)} %all-gather.5.cloned.1.call-done), kind=kOutput, calls=%fused_computation.7 | convolution fusion | flops 536870912 | bytes 3670016 | tf_op jit(solution)/shard_map/iap,jbp->iajb/dot_general | solution.py:55
  107.8 0.3 reshape.213
  108.1 0.8 copy.26
  109.0 0.3 copy.34
  109.2 4.5 %all-to-all-done.1 = f32[8,1,128,1,128]{4,2,3,1,0:T(8,128)S(1)} async-done(((f32[8,1,128,1,128]{4,2,3,1,0:T(8,128)}), f32[8,1,128,1,128]{4,2,3,1,0:T(8,128)S(1)}, u32[]{:S(2)}, u32[]{:S(2)}) %all-to-all-start.1) | async-done | bytes 524320 | tf_op jit(solution)/shard_map/all_to_all | solution.py:62
  113.7 3.5 %all-to-all-start = ((f32[8,1,128,1,128]{4,2,3,1,0:T(8,128)}), f32[8,1,128,1,128]{4,2,3,1,0:T(8,128)S(1)}, u32[]{:S(2)}, u32[]{:S(2)}) async-start(f32[8,1,128,1,128]{4,2,3,1,0:T(8,128)} %bitcast.118), calls=%async_computation | async-start | bytes 1048576 | tf_op jit(solution)/shard_map/all_to_all | solution.py:62
  117.2 3.9 %fusion.10 = f32[512,2048]{1,0:T(8,128)} fusion(bf16[1,256,2048]{2,1,0:T(8,128)(2,1)} %copy-done.1, f32[64,8,2,128]{3,2,1,0:T(2,128)S(1)} %bitcast.112, f32[512,256]{1,0:T(8,128)S(1)} %fusion.2, f32[512]{0:T(512)S(1)} %get-tuple-element.11, f32[256]{0:T(256)S(1)} %select_reduce_fusion.1), kind=kOutput, calls=%fused_computation.13 | convolution fusion | flops 537526272 | bytes 6294528 | tf_op jit(solution)/shard_map/iajb,jbp->iap/dot_general | solution.py:76
  121.2 0.3 copy.31
  121.4 0.0 collective-permute-done.2
  121.4 2.6 %fusion = f32[512,256]{1,0:T(8,128)S(1)} fusion(bf16[1,512,2048]{2,1,0:T(8,128)(2,1)} %all-gather.3.cloned.1.call-done, bf16[1,256,2048]{2,1,0:T(8,128)(2,1)} %collective-permute-done.2), kind=kOutput, calls=%fused_computation.1 | convolution fusion | flops 536870912 | bytes 3670016 | tf_op jit(solution)/shard_map/iap,jbp->iajb/dot_general | solution.py:55
  124.0 0.3 reshape.230
  124.3 0.8 copy.35
  125.1 0.9 all-to-all-done
  126.0 3.5 %all-to-all-start.3 = ((f32[8,1,128,1,128]{4,2,3,1,0:T(8,128)}), f32[8,1,128,1,128]{4,2,3,1,0:T(8,128)S(1)}, u32[]{:S(2)}, u32[]{:S(2)}) async-start(f32[8,1,128,1,128]{4,2,3,1,0:T(8,128)} %bitcast.29), calls=%async_computation.3 | async-start | bytes 1048576 | tf_op jit(solution)/shard_map/all_to_all | solution.py:62
  129.5 0.0 reduce-scatter.2.cloned.1.call-start
  129.6 4.0 %fusion.13 = f32[512,2048]{1,0:T(8,128)} fusion(bf16[1,256,2048]{2,1,0:T(8,128)(2,1)} %copy-done, f32[64,8,2,128]{3,2,1,0:T(2,128)S(1)} %bitcast.111, f32[512,256]{1,0:T(8,128)S(1)} %fusion.4, f32[512]{0:T(512)S(1)} %get-tuple-element.12, f32[256]{0:T(256)S(1)} %select_reduce_fusion.1), kind=kOutput, calls=%fused_computation.16 | convolution fusion | flops 537526272 | bytes 6294528 | tf_op jit(solution)/shard_map/iajb,jbp->iap/dot_general | solution.py:76
  133.6 0.3 copy.28
  133.8 4.0 %fusion.16 = f32[512,2048]{1,0:T(8,128)} fusion(bf16[1,256,2048]{2,1,0:T(8,128)(2,1)} %all-gather.5.cloned.1.call-done, f32[64,8,2,128]{3,2,1,0:T(2,128)S(1)} %bitcast.114, f32[512,256]{1,0:T(8,128)S(1)} %fusion.6, f32[256]{0:T(256)S(1)} %select_reduce_fusion.1, f32[512]{0:T(512)S(1)} %get-tuple-element.13), kind=kOutput, calls=%fused_computation.19 | convolution fusion | flops 537526272 | bytes 6294528 | tf_op jit(solution)/shard_map/iajb,jbp->iap/dot_general | solution.py:76
  137.8 0.5 all-to-all-done.3
  138.3 0.3 copy.37
  138.6 7.8 %add_bitcast_fusion = f32[1,512,2048]{2,1,0:T(8,128)} fusion(f32[512,2048]{1,0:T(8,128)} %fusion.10, f32[512,2048]{1,0:T(8,128)} %fusion.16, f32[512,2048]{1,0:T(8,128)} %fusion.13, bf16[1,256,2048]{2,1,0:T(8,128)(2,1)} %collective-permute-done.2, f32[64,8,2,128]{3,2,1,0:T(2,128)S(1)} %bitcast.113, f32[512,256]{1,0:T(8,128)S(1)} %fusion, ...), kind=kOutput, calls=%fused_computation | convolution fusion | flops 540672000 | bytes 18877440 | tf_op jit(solution)/shard_map/iajb,jbp->iap/dot_general | solution.py:76
  146.3 0.0 reduce-scatter.2.cloned.1.call-update
  146.4 42.8 %reduce-scatter.2.cloned.1.call-done = f32[1,128,2048]{2,1,0:T(8,128)} async-done(((f32[1,512,2048]{2,1,0:T(8,128)}), f32[1,128,2048]{2,1,0:T(8,128)}) %reduce-scatter.2.cloned.1.call-update) | async-done | bytes 1048592 | tf_op jit(solution)/shard_map/reduce_scatter | solution.py:79
  (9 shorter events, 0.0 us)
Async XLA Ops:
  6.5 26.4 %all-gather.5.cloned.1.call-start = ((), (), s32[]{:S(2)}) async-start(), calls=%async_computation.6 | async-start | bytes 1572864 | tf_op jit(solution)/shard_map/all_gather | solution.py:47
  7.3 78.1 %all-gather.3.cloned.1.call-start = ((), (), s32[]{:S(2)}) async-start(), calls=%async_computation.5 | async-start | bytes 2621440 | tf_op jit(solution)/shard_map/all_gather | solution.py:48
  32.9 26.7 %collective-permute-start = (bf16[1,256,2048]{2,1,0:T(8,128)(2,1)}, bf16[1,256,2048]{2,1,0:T(8,128)(2,1)S(1)}, u32[]{:S(2)}, u32[]{:S(2)}) collective-permute-start(bf16[1,256,2048]{2,1,0:T(8,128)(2,1)} %all-gather.5.cloned.1.call-done), channel_id=1, source_target_pairs={{24,0},{0,8},{8,16},{16,24},{25,1},{1,9},{9,17},{17,25},{26,2},{2,... | collective-permute-start | bytes 3145736 | tf_op jit(solution)/shard_map/ppermute | solution.py:12
  59.7 33.1 %copy-start = (bf16[1,256,2048]{2,1,0:T(8,128)(2,1)}, bf16[1,256,2048]{2,1,0:T(8,128)(2,1)S(1)}, u32[]{:S(2)}) copy-start(bf16[1,256,2048]{2,1,0:T(8,128)(2,1)S(1)} %collective-permute-done) | copy-start | bytes 3145732
  59.7 25.7 %collective-permute-start.1 = (bf16[1,256,2048]{2,1,0:T(8,128)(2,1)S(1)}, bf16[1,256,2048]{2,1,0:T(8,128)(2,1)S(1)}, u32[]{:S(2)}, u32[]{:S(2)}) collective-permute-start(bf16[1,256,2048]{2,1,0:T(8,128)(2,1)S(1)} %collective-permute-done), channel_id=1, source_target_pairs={{24,0},{0,8},{8,16},{16,24},{25,1},{1,9},{9,17},{17,25},{26,2},{2,... | collective-permute-start | bytes 3145736 | tf_op jit(solution)/shard_map/ppermute | solution.py:12
  85.3 2.7 %copy-start.1 = (bf16[1,256,2048]{2,1,0:T(8,128)(2,1)}, bf16[1,256,2048]{2,1,0:T(8,128)(2,1)S(1)}, u32[]{:S(2)}) copy-start(bf16[1,256,2048]{2,1,0:T(8,128)(2,1)S(1)} %collective-permute-done.1) | copy-start | bytes 3145732
  89.2 12.3 %all-to-all-start.2 = ((f32[8,1,128,1,128]{4,2,3,1,0:T(8,128)}), f32[8,1,128,1,128]{4,2,3,1,0:T(8,128)S(1)}, u32[]{:S(2)}, u32[]{:S(2)}) async-start(f32[8,1,128,1,128]{4,2,3,1,0:T(8,128)} %bitcast.22), calls=%async_computation.2 | async-start | bytes 1048576 | tf_op jit(solution)/shard_map/all_to_all | solution.py:62
  92.7 28.7 %collective-permute-start.2 = (bf16[1,256,2048]{2,1,0:T(8,128)(2,1)}, bf16[1,256,2048]{2,1,0:T(8,128)(2,1)}, u32[]{:S(2)}, u32[]{:S(2)}) collective-permute-start(bf16[1,256,2048]{2,1,0:T(8,128)(2,1)} %copy-done.1), channel_id=1, source_target_pairs={{24,0},{0,8},{8,16},{16,24},{25,1},{1,9},{9,17},{17,25},{26,2},{2,... | collective-permute-start | bytes 3145736 | tf_op jit(solution)/shard_map/ppermute | solution.py:12
  95.1 9.9 %copy-start.2 = (f32[1024]{0:T(1024)S(1)}, f32[1024]{0:T(1024)}, u32[]{:S(2)}) copy-start(f32[1024]{0:T(1024)} %param.7) | copy-start | bytes 12292
  101.5 12.3 %all-to-all-start.1 = ((f32[8,1,128,1,128]{4,2,3,1,0:T(8,128)}), f32[8,1,128,1,128]{4,2,3,1,0:T(8,128)S(1)}, u32[]{:S(2)}, u32[]{:S(2)}) async-start(f32[8,1,128,1,128]{4,2,3,1,0:T(8,128)} %bitcast.15), calls=%async_computation.1 | async-start | bytes 1048576 | tf_op jit(solution)/shard_map/all_to_all | solution.py:62
  113.7 12.3 %all-to-all-start = ((f32[8,1,128,1,128]{4,2,3,1,0:T(8,128)}), f32[8,1,128,1,128]{4,2,3,1,0:T(8,128)S(1)}, u32[]{:S(2)}, u32[]{:S(2)}) async-start(f32[8,1,128,1,128]{4,2,3,1,0:T(8,128)} %bitcast.118), calls=%async_computation | async-start | bytes 1048576 | tf_op jit(solution)/shard_map/all_to_all | solution.py:62
  126.0 12.3 %all-to-all-start.3 = ((f32[8,1,128,1,128]{4,2,3,1,0:T(8,128)}), f32[8,1,128,1,128]{4,2,3,1,0:T(8,128)S(1)}, u32[]{:S(2)}, u32[]{:S(2)}) async-start(f32[8,1,128,1,128]{4,2,3,1,0:T(8,128)} %bitcast.29), calls=%async_computation.3 | async-start | bytes 1048576 | tf_op jit(solution)/shard_map/all_to_all | solution.py:62
  129.5 59.6 %reduce-scatter.2.cloned.1.call-start = ((), (), s32[]{:S(2)}) async-start(), calls=%async_computation.7 | async-start | bytes 5242880 | tf_op jit(solution)/shard_map/reduce_scatter | solution.py:79
Sparse Core Ops, SparseCore 0:
  8.9 23.9 all-gather.4
  34.5 22.5 all-gather.2
  146.5 42.5 reduce-scatter.1
where the time goes:
time: 197 us; the launch traced here: 196 us
  waiting for transfers between devices  118 us (60%)
  matrix products  29.9 us (15%)
  between operations  18.3 us (9%)
  starting transfers between devices  15.6 us (8%)
  local copies, waits for them, and re-layouts  8.41 us (4%)
  other arithmetic  5.74 us (3%)
    reduce_scatter x1, waiting for transfers between devices, per_device(): return lax.psum_scatter(gradient, 'vb', scatter_dimension=1, tiled=True)  42.8 us
    ppermute x3, waiting for transfers between devices, passed_along(): return lax.ppermute(block, axis, route)  37.5 us
    all_gather x1, waiting for transfers between devices, per_device(): own_columns = lax.all_gather(aux_factors, 'va', axis=1, tiled=True)  24.9 us
    dot_general x4, matrix products, per_device(): jnp.einsum('iajb,jbp->iap', weights, far_columns, preferred_element_type=...  19.6 us
    all_to_all x4, starting transfers between devices, per_device(): lax.all_to_all(outgoing, ('va', 'vb'), split_axis=0, concat_axis=0, tiled...  14 us
    all_to_all x4, waiting for transfers between devices, per_device(): lax.all_to_all(outgoing, ('va', 'vb'), split_axis=0, concat_axis=0, tiled...  11.1 us
    dot_general x4, matrix products, per_device(): jnp.einsum('iap,jbp->iajb', own_rows, far_columns, preferred_element_type...  10.2 us
    reduce_sum x3, other arithmetic, lookup(): return jnp.sum(jnp.where(matches, energies[None, :], 0.0), axis=1)  5.73 us
  transfers between devices with their start and end apart: 10, of which 8 were waited for; matrix products, arithmetic and copies ran while one was open for 16% of the time, Pallas kernels for 0%

commit v1 on v0

--- a/solution.py
+++ b/solution.py
@@ -44,7 +44,9 @@
         )
 
     own_energy = block_energy(occ_rank)
-    own_columns = lax.all_gather(aux_factors, "va", axis=1, tiled=True)
+    own_columns = jnp.concatenate(
+        lax.all_to_all(jnp.stack([aux_factors] * lax.axis_size("va")), "va", 0, 0), axis=1
+    )
     own_rows = lax.all_gather(aux_factors, "vb", axis=1, tiled=True)
     gradient = jnp.zeros((occ_rows, row_count, aux_width), jnp.float32)
     far_columns = own_columns

time: 197 us -> 184 us (0.934)
  waiting for transfers between devices: 118 us -> 83 us
  blocking collectives: 0 us -> 17.6 us
  local copies, waits for them, and re-layouts: 8.41 us -> 11.8 us
    all_gather x1 -> x0, waiting for transfers between devices: 24.9 us -> none  [per_device(): own_columns = lax.all_gather(aux_factors, 'va', axis=1, tiled=True)]
    all_to_all x0 -> x1, blocking collectives: none -> 17.6 us  [per_device(): lax.all_to_all(jnp.stack([aux_factors] * lax.axis_size('va')), 'va', 0, 0)]
    all_to_all x4, waiting for transfers between devices: 11.1 us -> 2.74 us  [per_device(): lax.all_to_all(outgoing, ('va', 'vb'), split_axis=0, concat_axis=0, tiled...]
    ppermute x3, waiting for transfers between devices: 37.5 us -> 33 us  [passed_along(): return lax.ppermute(block, axis, route)]
    reduce_scatter x1, waiting for transfers between devices: 42.8 us -> 46.5 us  [per_device(): return lax.psum_scatter(gradient, 'vb', scatter_dimension=1, tiled=True)]
    transpose x4, local copies, waits for them, and re-layouts: 1.01 us -> 4.48 us  [per_device(): incoming.transpose(2, 1, 5, 4, 0, 3)]
    reshape x8, local copies, waits for them, and re-layouts: 4.43 us -> 6.66 us  [per_device(): kernel.reshape(occ_rows, vb_count, block_width, occ_rows, va_count, block...]
  transfers between devices with their start and end apart: 10 -> 9, of which waited for: 8 -> 5; matrix products, arithmetic and copies ran while one was open for 16% -> 21% of each run, Pallas kernels for 0% -> 0%
where the time goes in v1:
time: 184 us; the launch traced here: 183 us
  waiting for transfers between devices  83 us (45%)
  matrix products  28.6 us (16%)
  between operations  18.7 us (10%)
  blocking collectives  17.6 us (10%)
  starting transfers between devices  17.1 us (9%)
  local copies, waits for them, and re-layouts  11.8 us (6%)
  other arithmetic  5.73 us (3%)
    reduce_scatter x1, waiting for transfers between devices, per_device(): return lax.psum_scatter(gradient, 'vb', scatter_dimension=1, tiled=True)  46.5 us
    ppermute x3, waiting for transfers between devices, passed_along(): return lax.ppermute(block, axis, route)  33 us
    dot_general x4, matrix products, per_device(): jnp.einsum('iajb,jbp->iap', weights, far_columns, preferred_element_type=...  18.8 us
    all_to_all x1, blocking collectives, per_device(): lax.all_to_all(jnp.stack([aux_factors] * lax.axis_size('va')), 'va', 0, 0)  17.6 us
    all_to_all x4, starting transfers between devices, per_device(): lax.all_to_all(outgoing, ('va', 'vb'), split_axis=0, concat_axis=0, tiled...  15.3 us
    dot_general x4, matrix products, per_device(): jnp.einsum('iap,jbp->iajb', own_rows, far_columns, preferred_element_type...  9.77 us
    reshape x8, local copies, waits for them, and re-layouts, per_device(): kernel.reshape(occ_rows, vb_count, block_width, occ_rows, va_count, block...  6.66 us
    transpose x4, local copies, waits for them, and re-layouts, per_device(): incoming.transpose(2, 1, 5, 4, 0, 3)  4.48 us
  transfers between devices with their start and end apart: 9, of which 5 were waited for; matrix products, arithmetic and copies ran while one was open for 21% of the time, Pallas kernels for 0%

profile of v1, /device:TPU:0, one launch (start us, length us, event | category | flops | bytes accessed | tf_op | source)
XLA Modules:
  0.0 182.6 jit_solution(5890638022721219750)
XLA Ops:
  6.5 0.0 all-gather.2.cloned.1.call-start
  6.6 0.7 all-gather.2.cloned.1.call-update
  7.3 1.4 pad_maximum_fusion
  8.7 17.6 %all_to_all.25 = bf16[2,1,128,2048]{3,2,1,0:T(8,128)(2,1)S(1)} all-to-all(bf16[2,1,128,2048]{3,2,1,0:T(8,128)(2,1)S(1)} %pad_maximum_fusion), channel_id=1, replica_groups=mesh['occ'=4,'va'=2,'vb'=4] {'va'}, dimensions={0} | all-to-all | bytes 2097152 | tf_op jit(solution)/shard_map/all_to_all | solution.py:48
  26.3 1.8 collective-permute-start
  28.0 24.4 %collective-permute-done = bf16[1,256,2048]{2,1,0:T(8,128)(2,1)} collective-permute-done((bf16[1,256,2048]{2,1,0:T(8,128)(2,1)S(1)}, bf16[1,256,2048]{2,1,0:T(8,128)(2,1)}, u32[]{:S(2)}, u32[]{:S(2)}) %collective-permute-start) | collective-permute-done | bytes 1048608 | tf_op jit(solution)/shard_map/ppermute | solution.py:12
  52.5 0.0 collective-permute-start.1
  52.5 0.0 copy-done.2
  52.5 0.7 fusion.62
  53.1 3.7 %fusion.57 = (f32[]{:T(128)}, f32[]{:T(128)}, f32[]{:T(128)}, f32[]{:T(128)}, f32[]{:T(128)}) fusion(f32[4]{0:T(128)S(1)} %copy-done.4, s32[]{:T(128)} %bitcast.38, s32[]{:T(128)} %bitcast.22, s32[]{:T(128)} %bitcast.10, s32[]{:T(128)} %bitcast.9, s32[]{:T(128)} %bitcast.30), kind=kLoop, calls=%fused_computation.64 | loop fusion | flops 55 | bytes 56 | tf_op jit(solution)/shard_map/reduce_sum | solution.py:18
  62.0 0.0 copy-done.1
  62.0 0.4 select_reduce_fusion
  62.3 0.0 all-gather.2.cloned.1.call-done
  62.4 2.3 %fusion.8 = f32[512,256]{0,1:T(8,128)S(1)} fusion(bf16[256,2048]{1,0:T(8,128)(2,1)S(1)} %bitcast.140, bf16[1,512,2048]{2,1,0:T(8,128)(2,1)} %all-gather.2.cloned.1.call-done), kind=kOutput, calls=%fused_computation.11 | convolution fusion | flops 536870912 | bytes 3670016 | tf_op jit(solution)/shard_map/iap,jbp->iajb/dot_general | solution.py:57
  64.7 0.2 reshape.218
  64.9 1.0 copy.26
  65.9 3.5 %all-to-all-start.1 = ((f32[8,1,128,1,128]{4,2,3,1,0:T(8,128)}), f32[8,1,128,1,128]{4,2,3,1,0:T(8,128)S(1)}, u32[]{:S(2)}, u32[]{:S(2)}) async-start(f32[8,1,128,1,128]{4,2,3,1,0:T(8,128)} %bitcast.6), calls=%async_computation.1 | async-start | bytes 1048576 | tf_op jit(solution)/shard_map/all_to_all | solution.py:64
  69.4 8.6 %collective-permute-done.1 = bf16[1,256,2048]{2,1,0:T(8,128)(2,1)} collective-permute-done((bf16[1,256,2048]{2,1,0:T(8,128)(2,1)}, bf16[1,256,2048]{2,1,0:T(8,128)(2,1)}, u32[]{:S(2)}, u32[]{:S(2)}) %collective-permute-start.1) | collective-permute-done | bytes 1048608 | tf_op jit(solution)/shard_map/ppermute | solution.py:12
  78.0 0.0 collective-permute-start.2
  78.0 2.6 %fusion.14 = f32[512,256]{0,1:T(8,128)S(1)} fusion(bf16[1,512,2048]{2,1,0:T(8,128)(2,1)} %all-gather.2.cloned.1.call-done, bf16[1,256,2048]{2,1,0:T(8,128)(2,1)} %collective-permute-done.1), kind=kOutput, calls=%fused_computation.13 | convolution fusion | flops 536870912 | bytes 3670016 | tf_op jit(solution)/shard_map/iap,jbp->iajb/dot_general | solution.py:57
  80.7 0.2 reshape.231
  80.9 1.0 copy.32
  81.9 0.0 all-to-all-done.1
  81.9 4.2 %all-to-all-start.3 = ((f32[8,1,128,1,128]{4,2,3,1,0:T(8,128)}), f32[8,1,128,1,128]{4,2,3,1,0:T(8,128)}, u32[]{:S(2)}, u32[]{:S(2)}) async-start(f32[8,1,128,1,128]{4,2,3,1,0:T(8,128)} %bitcast.27), calls=%async_computation.3 | async-start | bytes 1048576 | tf_op jit(solution)/shard_map/all_to_all | solution.py:64
  86.1 0.2 select_reduce_fusion.1
  86.3 2.7 %fusion.11 = f32[512,256]{0,1:T(8,128)S(1)} fusion(bf16[1,512,2048]{2,1,0:T(8,128)(2,1)} %all-gather.2.cloned.1.call-done, bf16[1,256,2048]{2,1,0:T(8,128)(2,1)} %collective-permute-done), kind=kOutput, calls=%fused_computation.12 | convolution fusion | flops 536870912 | bytes 3670016 | tf_op jit(solution)/shard_map/iap,jbp->iajb/dot_general | solution.py:57
  89.0 1.0 reshape.226
  90.0 2.1 %copy.29 = f32[1,4,128,1,2,128]{5,2,1,4,3,0:T(8,128)} copy(f32[1,4,128,1,2,128]{2,1,5,4,3,0:T(4,128)} %reshape.226) | data formatting | bytes 1048576 | tf_op jit(solution)/shard_map/reshape | solution.py:60
  92.1 1.4 copy.28
  93.5 1.4 all-to-all-done.3
  94.9 4.1 %all-to-all-start.2 = ((f32[8,1,128,1,128]{4,2,3,1,0:T(8,128)}), f32[8,1,128,1,128]{4,2,3,1,0:T(8,128)}, u32[]{:S(2)}, u32[]{:S(2)}) async-start(f32[8,1,128,1,128]{4,2,3,1,0:T(8,128)} %bitcast.148), calls=%async_computation.2 | async-start | bytes 1048576 | tf_op jit(solution)/shard_map/all_to_all | solution.py:64
  99.1 2.8 %fusion.36 = f32[512,2048]{1,0:T(8,128)} fusion(bf16[256,2048]{1,0:T(8,128)(2,1)S(1)} %bitcast.141, f32[32,8,4,128]{3,2,1,0:T(4,128)S(1)} %bitcast.143, f32[512,256]{0,1:T(8,128)S(1)} %fusion.8, f32[256]{0:T(256)S(1)} %select_reduce_fusion.1, f32[512]{0:T(512)S(1)} %get-tuple-element.13), kind=kOutput, calls=%fused_computation.38 | convolution fusion | flops 537526272 | bytes 6294528 | tf_op jit(solution)/shard_map/iajb,jbp->iap/dot_general | solution.py:78
  101.9 1.4 copy.34
  103.2 0.0 collective-permute-done.2
  103.3 2.1 %fusion.17 = f32[512,256]{0,1:T(8,128)S(1)} fusion(bf16[1,512,2048]{2,1,0:T(8,128)(2,1)S(1)} %copy-done.5, bf16[1,256,2048]{2,1,0:T(8,128)(2,1)} %collective-permute-done.2), kind=kOutput, calls=%fused_computation.14 | convolution fusion | flops 536870912 | bytes 3670016 | tf_op jit(solution)/shard_map/iap,jbp->iajb/dot_general | solution.py:57
  105.4 0.2 reshape.236
  105.6 1.0 copy.35
  106.6 1.3 all-to-all-done.2
  107.9 3.5 %all-to-all-start.4 = ((f32[8,1,128,1,128]{4,2,3,1,0:T(8,128)}), f32[8,1,128,1,128]{4,2,3,1,0:T(8,128)S(1)}, u32[]{:S(2)}, u32[]{:S(2)}) async-start(f32[8,1,128,1,128]{4,2,3,1,0:T(8,128)} %bitcast.35), calls=%async_computation.4 | async-start | bytes 1048576 | tf_op jit(solution)/shard_map/all_to_all | solution.py:64
  111.4 0.0 reduce-scatter.2.cloned.1.call-start
  111.5 4.1 %fusion.22 = f32[512,2048]{1,0:T(8,128)} fusion(bf16[1,256,2048]{2,1,0:T(8,128)(2,1)} %collective-permute-done.1, f32[32,8,4,128]{3,2,1,0:T(4,128)S(1)} %bitcast.142, f32[512,256]{0,1:T(8,128)S(1)} %fusion.14, f32[512]{0:T(512)S(1)} %get-tuple-element.11, f32[256]{0:T(256)S(1)} %select_reduce_fusion.1), kind=kOutput, calls=%fused_computation.18 | convolution fusion | flops 537526272 | bytes 6294528 | tf_op jit(solution)/shard_map/iajb,jbp->iap/dot_general | solution.py:78
  115.5 1.4 copy.31
  116.9 4.1 %fusion.25 = f32[512,2048]{1,0:T(8,128)} fusion(bf16[1,256,2048]{2,1,0:T(8,128)(2,1)} %collective-permute-done, f32[32,8,4,128]{3,2,1,0:T(4,128)S(1)} %bitcast.144, f32[512,256]{0,1:T(8,128)S(1)} %fusion.11, f32[512]{0:T(512)S(1)} %get-tuple-element.12, f32[256]{0:T(256)S(1)} %select_reduce_fusion.1), kind=kOutput, calls=%fused_computation.21 | convolution fusion | flops 537526272 | bytes 6294528 | tf_op jit(solution)/shard_map/iajb,jbp->iap/dot_general | solution.py:78
  121.0 0.0 all-to-all-done.4
  121.0 0.3 copy.37
  121.3 7.9 %add_bitcast_fusion = f32[1,512,2048]{2,1,0:T(8,128)} fusion(f32[512,2048]{1,0:T(8,128)} %fusion.22, f32[512,2048]{1,0:T(8,128)} %fusion.36, f32[512,2048]{1,0:T(8,128)} %fusion.25, bf16[1,256,2048]{2,1,0:T(8,128)(2,1)} %collective-permute-done.2, f32[32,8,4,128]{3,2,1,0:T(4,128)S(1)} %bitcast.146, f32[512,256]{0,1:T(8,128)S(1)} %fusion.17, ...), kind=kOutput, calls=%fused_computation | convolution fusion | flops 540672000 | bytes 18877440 | tf_op jit(solution)/shard_map/iajb,jbp->iap/dot_general | solution.py:78
  129.2 0.0 reduce-scatter.2.cloned.1.call-update
  129.2 46.5 %reduce-scatter.2.cloned.1.call-done = f32[1,128,2048]{2,1,0:T(8,128)} async-done(((f32[1,512,2048]{2,1,0:T(8,128)}), f32[1,128,2048]{2,1,0:T(8,128)}) %reduce-scatter.2.cloned.1.call-update) | async-done | bytes 1048592 | tf_op jit(solution)/shard_map/reduce_scatter | solution.py:81
  (14 shorter events, 0.1 us)
Async XLA Ops:
  6.5 45.9 %copy-start.2 = (s32[4]{0:T(128)S(1)}, s32[4]{0:T(128)}, u32[]{:S(2)}) copy-start(s32[4]{0:T(128)} %param.8) | copy-start | bytes 52
  6.5 46.6 %copy-start.4 = (f32[4]{0:T(128)S(1)}, f32[4]{0:T(128)}, u32[]{:S(2)}) copy-start(f32[4]{0:T(128)} %param.6) | copy-start | bytes 52
  6.5 55.4 %copy-start.3 = (s32[1024]{0:T(1024)S(1)}, s32[1024]{0:T(1024)}, u32[]{:S(2)}) copy-start(s32[1024]{0:T(1024)} %param.9) | copy-start | bytes 12292
  6.5 55.4 %copy-start.1 = (f32[1024]{0:T(1024)S(1)}, f32[1024]{0:T(1024)}, u32[]{:S(2)}) copy-start(f32[1024]{0:T(1024)} %param.7) | copy-start | bytes 12292
  6.5 55.8 %all-gather.2.cloned.1.call-start = ((), (), s32[]{:S(2)}) async-start(), calls=%async_computation.6 | async-start | bytes 2621440 | tf_op jit(solution)/shard_map/all_gather | solution.py:50
  26.3 26.2 %collective-permute-start = (bf16[1,256,2048]{2,1,0:T(8,128)(2,1)S(1)}, bf16[1,256,2048]{2,1,0:T(8,128)(2,1)}, u32[]{:S(2)}, u32[]{:S(2)}) collective-permute-start(bf16[1,256,2048]{2,1,0:T(8,128)(2,1)S(1)} %bitcast.139), channel_id=1, source_target_pairs={{24,0},{0,8},{8,16},{16,24},{25,1},{1,9},{9,17},{17,25},{26,2},{2,... | collective-permute-start | bytes 3145736 | tf_op jit(solution)/shard_map/ppermute | solution.py:12
  52.5 25.5 %collective-permute-start.1 = (bf16[1,256,2048]{2,1,0:T(8,128)(2,1)}, bf16[1,256,2048]{2,1,0:T(8,128)(2,1)}, u32[]{:S(2)}, u32[]{:S(2)}) collective-permute-start(bf16[1,256,2048]{2,1,0:T(8,128)(2,1)} %collective-permute-done), channel_id=1, source_target_pairs={{24,0},{0,8},{8,16},{16,24},{25,1},{1,9},{9,17},{17,25},{26,2},{2,... | collective-permute-start | bytes 3145736 | tf_op jit(solution)/shard_map/ppermute | solution.py:12
  65.9 16.0 %all-to-all-start.1 = ((f32[8,1,128,1,128]{4,2,3,1,0:T(8,128)}), f32[8,1,128,1,128]{4,2,3,1,0:T(8,128)S(1)}, u32[]{:S(2)}, u32[]{:S(2)}) async-start(f32[8,1,128,1,128]{4,2,3,1,0:T(8,128)} %bitcast.6), calls=%async_computation.1 | async-start | bytes 1048576 | tf_op jit(solution)/shard_map/all_to_all | solution.py:64
  78.0 25.2 %collective-permute-start.2 = (bf16[1,256,2048]{2,1,0:T(8,128)(2,1)}, bf16[1,256,2048]{2,1,0:T(8,128)(2,1)}, u32[]{:S(2)}, u32[]{:S(2)}) collective-permute-start(bf16[1,256,2048]{2,1,0:T(8,128)(2,1)} %collective-permute-done.1), channel_id=1, source_target_pairs={{24,0},{0,8},{8,16},{16,24},{25,1},{1,9},{9,17},{17,25},{26,2},{2,... | collective-permute-start | bytes 3145736 | tf_op jit(solution)/shard_map/ppermute | solution.py:12
  81.9 7.1 %copy-start = (f32[8,1,128,1,128]{4,2,3,1,0:T(8,128)}, f32[8,1,128,1,128]{4,2,3,1,0:T(8,128)S(1)}, u32[]{:S(2)}) copy-start(f32[8,1,128,1,128]{4,2,3,1,0:T(8,128)S(1)} %all-to-all-done.1) | copy-start | bytes 1572868
  81.9 13.0 %all-to-all-start.3 = ((f32[8,1,128,1,128]{4,2,3,1,0:T(8,128)}), f32[8,1,128,1,128]{4,2,3,1,0:T(8,128)}, u32[]{:S(2)}, u32[]{:S(2)}) async-start(f32[8,1,128,1,128]{4,2,3,1,0:T(8,128)} %bitcast.27), calls=%async_computation.3 | async-start | bytes 1048576 | tf_op jit(solution)/shard_map/all_to_all | solution.py:64
  94.9 13.0 %all-to-all-start.2 = ((f32[8,1,128,1,128]{4,2,3,1,0:T(8,128)}), f32[8,1,128,1,128]{4,2,3,1,0:T(8,128)}, u32[]{:S(2)}, u32[]{:S(2)}) async-start(f32[8,1,128,1,128]{4,2,3,1,0:T(8,128)} %bitcast.148), calls=%async_computation.2 | async-start | bytes 1048576 | tf_op jit(solution)/shard_map/all_to_all | solution.py:64
  99.0 4.2 %copy-start.5 = (bf16[1,512,2048]{2,1,0:T(8,128)(2,1)S(1)}, bf16[1,512,2048]{2,1,0:T(8,128)(2,1)}, u32[]{:S(2)}) copy-start(bf16[1,512,2048]{2,1,0:T(8,128)(2,1)} %all-gather.2.cloned.1.call-done) | copy-start | bytes 6291460
  107.9 13.1 %all-to-all-start.4 = ((f32[8,1,128,1,128]{4,2,3,1,0:T(8,128)}), f32[8,1,128,1,128]{4,2,3,1,0:T(8,128)S(1)}, u32[]{:S(2)}, u32[]{:S(2)}) async-start(f32[8,1,128,1,128]{4,2,3,1,0:T(8,128)} %bitcast.35), calls=%async_computation.4 | async-start | bytes 1048576 | tf_op jit(solution)/shard_map/all_to_all | solution.py:64
  111.4 64.4 %reduce-scatter.2.cloned.1.call-start = ((), (), s32[]{:S(2)}) async-start(), calls=%async_computation.7 | async-start | bytes 5242880 | tf_op jit(solution)/shard_map/reduce_scatter | solution.py:81
Sparse Core Ops, SparseCore 0:
  8.9 25.2 all-gather.1
  129.3 46.3 reduce-scatter.1
